TPU v7x, 32 devices: a whole 2x2x4 slice. The times are simulated.
32 devices in a mesh: station: 4 (over z), group: 4 (over x, core), bias: 2 (over y).
Axes of the slice: x: 2, y: 2, z: 4, core: 2. Of those that a mesh axis runs over, the one named last changes fastest.
Arguments:
- normal_mat: float32 [128, 2304], P(('station', 'group')), may hold values from -16 to 18, as said below
- coupling: float32 [128, 2, 8, 48, 128], P(('station', 'group'), 'bias'), may hold values from -0.13258252 to 0.13258252
- lengths: int32 [128], P(('station', 'group')), may hold values from 12 to 48
- visible: int32 [128, 2, 8], P(('station', 'group'), 'bias'), may hold values from 0 to 16, as said below
- bias_prior: float32 [2, 16, 128], P('bias', 'station'), may hold values from 0.1 to 1
- unimod: int32 [128, 2304], P(('station', 'group')), may hold values from -1 to 2, as said below
Outputs:
- bias_cov: float32 [2, 16, 128, 128], P('bias', 'station')
- amb_cov: float32 [128, 2304], P(('station', 'group'))
Inputs may be any that keep to these rules, and one draw needn't show every extreme that they name: `normal_mat`: each station's matrix, read as 48 x 48 row by row, is symmetric with all eigenvalues 1 or more. Each list visible[s, h] holds distinct block numbers below 16 in its first slots and the value 16 in its unused slots; every list has at least one block; in every draw the stations of some devices use all 8 slots. `unimod`: each station's matrix, read as 48 x 48 row by row, is a unit lower triangular times a unit upper triangular integer matrix; each row of the lower factor and each column of the upper factor holds at most one entry off the diagonal, -1 or 1; so every leading square block has determinant 1.
All inputs are finite; a program needn't handle non-finite values.
Results may differ from a plain program's by a relative error of at most 0.0003.
Values sent between devices are 32-bit elements; how exact they have to be, the bound alone decides.
No kernel may reach another device: no remote copies, remote signals or barrier semaphores. Data moves between devices by JAX's collectives and lax.ppermute only.
A program may use at most 64 MiB of HBM per device.

v0:
```python
import jax
import jax.numpy as jnp
from jax import lax
from jax.sharding import PartitionSpec as P

NHALF = 16
precise = lax.Precision.HIGHEST


def spd_inverse(matrix):
    matrix_order = matrix.shape[-1]
    factor = jnp.linalg.cholesky(matrix)
    identity = jnp.broadcast_to(jnp.eye(matrix_order, dtype=matrix.dtype), matrix.shape)
    lower_inv = lax.linalg.triangular_solve(factor, identity, left_side=True, lower=True)
    return jnp.einsum("...ka,...kb->...ab", lower_inv, lower_inv, precision=precise)


def prepare(normal_mat, coupling, lengths):
    stations = coupling.shape[0]
    block_len = coupling.shape[3]
    positions = jnp.arange(block_len, dtype=jnp.int32)
    row_valid = (positions[None, :] < lengths[:, None]).astype(jnp.float32)
    keep_mask = row_valid[:, :, None] * row_valid[:, None, :]
    stacked = normal_mat.reshape(stations, block_len, block_len)
    effective = keep_mask * stacked + (1.0 - keep_mask) * jnp.eye(block_len, dtype=jnp.float32)
    inverse = spd_inverse(effective)
    weighted = coupling * row_valid[:, None, None, :, None]
    solved = jnp.einsum("sab,shjbc->shjac", inverse, weighted, precision=precise)
    return (keep_mask, inverse, weighted, solved)


def finish_cov(keep_mask, inverse, bias_part, unimod):
    stations = keep_mask.shape[0]
    block_len = keep_mask.shape[1]
    covariance = keep_mask * (inverse + bias_part)
    integer_map = unimod.reshape(stations, block_len, block_len).astype(jnp.float32)
    mapped = jnp.einsum("sab,sbc,sdc->sad", integer_map, covariance, integer_map, precision=precise)
    return (keep_mask * mapped).reshape(stations, block_len * block_len)


def local(normal_mat, coupling, lengths, visible, bias_prior, unimod):
    keep_mask, inverse, weighted, solved = prepare(normal_mat, coupling, lengths)
    reduced = jnp.einsum("shjac,shjad->shjcd", weighted, weighted - solved, precision=precise)
    block_width = coupling.shape[4]
    identity = jnp.eye(block_width, dtype=jnp.float32)
    columns = jnp.arange(NHALF, dtype=jnp.int32)
    selector = (visible[..., None] == columns).astype(jnp.float32)
    block_table = jnp.einsum("shjx,shjcd->hxcd", selector, reduced, precision=precise)
    local_sum = lax.psum_scatter(block_table, "station", scatter_dimension=1, tiled=True)
    block_sum = lax.psum(local_sum, "group")
    bias_cov = spd_inverse(block_sum + bias_prior[..., :, None] * identity)
    segment = lax.all_gather(bias_cov, "station", axis=1, tiled=True)
    piece_len = segment.shape[1]
    local_pick = (visible[..., None] == jnp.arange(piece_len, dtype=jnp.int32)).astype(jnp.float32)
    chosen = jnp.einsum("shjx,hxcd->shjcd", local_pick, segment, precision=precise)
    lifted = jnp.einsum("shjac,shjcd->shjad", solved, chosen, precision=precise)
    bias_part = jnp.einsum("shjad,shjbd->sab", lifted, solved, precision=precise)
    combined = lax.psum(bias_part.reshape(bias_part.shape[0], -1), "bias")
    amb_cov = finish_cov(keep_mask, inverse, combined.reshape(bias_part.shape), unimod)
    return (bias_cov, amb_cov)


def solution(mesh):
    return jax.shard_map(
        local,
        mesh=mesh,
        in_specs=(
            P(("station", "group"), None),
            P(("station", "group"), "bias", None, None, None),
            P(("station", "group")),
            P(("station", "group"), "bias", None),
            P("bias", "station", None),
            P(("station", "group"), None),
        ),
        out_specs=(P("bias", "station", None, None), P(("station", "group"), None)),
        check_vma=False,
    )
```

profile of v0, /device:TPU:0, one launch (start us, length us, event | category | flops | bytes accessed | tf_op | source)
XLA Modules:
  0.0 314.8 jit_solution(5613608994066356341)
XLA Ops:
  7.2 0.0 reduce-scatter.2.cloned.1.call-start
  7.3 0.7 fusion.43
  8.0 0.1 copy.56
  8.1 1.0 reshape.177
  9.1 0.1 copy.55
  9.2 0.1 fusion.24
  9.3 0.1 copy.57
  9.4 0.1 fusion.30
  9.6 35.2 %custom-call.14 = f32[8,48,48]{2,1,0:T(8,128)S(1)} custom-call(f32[8,48,48]{2,1,0:T(8,128)S(1)} %fusion.30), custom_call_target="Cholesky" | custom-call | tf_op jit(solution)/shard_map/jit(cholesky)/cholesky | solution.py:12
  44.8 0.1 compare_reduce_fusion
  44.9 0.1 select_bitcast_fusion.1
  45.0 29.5 %custom-call.15 = f32[8,1,48,48]{2,3,1,0:T(8,128)S(1)} custom-call(f32[8,1,48,48]{3,2,1,0:T(8,128)S(1)} %select_bitcast_fusion.1), custom_call_target="InvertDiagBlocksLowerTriangular" | custom-call | tf_op jit(solution)/shard_map/triangular_solve | solution.py:14
  74.6 0.5 fusion.28
  75.1 0.5 fusion.44
  75.6 1.7 fusion.10
  77.3 6.9 %fusion.7 = f32[8,8,128,128]{3,2,1,0:T(8,128)S(1)} fusion(f32[8,8,128,48]{2,3,1,0:T(8,128)S(1)} %fusion.10, f32[8,1,8,48,128]{4,3,2,1,0:T(8,128)S(1)} %copy-done, f32[8,48]{1,0:T(8,128)S(1)} %fusion.43), kind=kOutput, calls=%fused_computation.9 | convolution fusion | flops 605159424 | bytes 7341568 | tf_op jit(solution)/shard_map/shjac,shjad->shjcd/dot_general | solution.py:43
  84.2 4.1 %fusion.12 = f32[16,128,128]{2,0,1:T(8,128)S(1)} fusion(f32[8,8,128,128]{3,2,1,0:T(8,128)S(1)} %fusion.7, s32[8,8]{1,0:T(8,128)S(1)} %bitcast.86), kind=kOutput, calls=%fused_computation.14 | convolution fusion | flops 201327616 | bytes 5243136 | tf_op jit(solution)/shard_map/shjx,shjcd->hxcd/dot_general | solution.py:48
  88.3 1.4 copy.62
  89.8 0.0 reduce-scatter.2.cloned.1.call-update
  89.8 0.0 all-reduce.3.cloned.1.call-start
  89.9 30.1 %reduce-scatter.2.cloned.1.call-done = f32[1,4,128,128]{2,3,1,0:T(8,128)} async-done(((f32[1,16,128,128]{2,3,1,0:T(8,128)}), f32[1,4,128,128]{2,3,1,0:T(8,128)}) %reduce-scatter.2.cloned.1.call-update) | async-done | bytes 262160 | tf_op jit(solution)/shard_map/reduce_scatter | solution.py:49
  120.0 0.0 all-reduce.3.cloned.1.call-update
  120.0 0.0 all-gather.3.cloned.1.call-start
  120.1 0.1 copy.63
  120.2 32.9 %all-reduce.3.cloned.1.call-done = f32[1,4,128,128]{2,3,1,0:T(8,128)} async-done(((f32[1,4,128,128]{2,3,1,0:T(8,128)}), f32[1,4,128,128]{2,3,1,0:T(8,128)}) %all-reduce.3.cloned.1.call-update) | async-done | bytes 262160 | tf_op jit(solution)/shard_map/psum | solution.py:50
  153.1 1.0 multiply_add_fusion
  154.1 0.1 copy.64
  154.2 1.0 fusion.23
  155.3 46.9 %custom-call.16 = f32[1,4,128,128]{3,2,1,0:T(8,128)S(1)} custom-call(f32[1,4,128,128]{3,2,1,0:T(8,128)S(1)} %fusion.23), custom_call_target="Cholesky" | custom-call | tf_op jit(solution)/shard_map/jit(cholesky)/cholesky | solution.py:12
  202.2 0.1 compare_reduce_fusion.1
  202.3 0.1 select_bitcast_fusion
  202.4 39.3 %custom-call.17 = f32[1,4,1,128,128]{3,4,2,1,0:T(8,128)S(1)} custom-call(f32[1,4,1,128,128]{4,3,2,1,0:T(8,128)S(1)} %select_bitcast_fusion), custom_call_target="InvertDiagBlocksLowerTriangular" | custom-call | tf_op jit(solution)/shard_map/triangular_solve | solution.py:14
  241.8 0.6 fusion.21
  242.3 1.3 fusion.45
  243.7 0.0 all-gather.3.cloned.1.call-update
  243.7 0.3 all-reduce.5.cloned.1.call-start
  243.9 27.9 %all-gather.3.cloned.1.call-done = f32[16,128,128]{2,1,0:T(8,128)} async-done(((f32[4,128,128]{2,1,0:T(8,128)}), f32[16,128,128]{2,1,0:T(8,128)}) %all-gather.3.cloned.1.call-update) | async-done | bytes 1048592 | tf_op jit(solution)/shard_map/all_gather | solution.py:52
  271.8 3.3 %convolution_bitcast_fusion = f32[8,8,128,128]{3,1,0,2:T(8,128)S(1)} fusion(f32[16,128,128,1]{2,1,0,3:T(8,128)} %bitcast.85, s32[8,8]{1,0:T(8,128)S(1)} %bitcast.87), kind=kOutput, calls=%fused_computation.4 | convolution fusion | flops 201327616 | bytes 5243136 | tf_op jit(solution)/shard_map/shjx,hxcd->shjcd/dot_general | solution.py:55
  275.1 6.0 %fusion = f32[8,8,48,128]{3,2,1,0:T(8,128)S(1)} fusion(f32[8,8,128,48]{2,3,1,0:T(8,128)S(1)} %fusion.10, f32[8,8,128,128]{3,1,0,2:T(8,128)S(1)} %convolution_bitcast_fusion), kind=kOutput, calls=%fused_computation | convolution fusion | flops 603979776 | bytes 7340032 | tf_op jit(solution)/shard_map/shjac,shjcd->shjad/dot_general | solution.py:56
  281.1 2.4 fusion.15
  283.5 0.0 all-reduce.5.cloned.1.call-update
  283.5 0.1 copy.70
  283.7 0.1 convert_element_type.47
  283.8 21.7 %all-reduce.5.cloned.1.call-done = f32[8,48,48]{1,2,0:T(8,128)} async-done(((f32[8,48,48]{1,2,0:T(8,128)}), f32[8,48,48]{1,2,0:T(8,128)}) %all-reduce.5.cloned.1.call-update) | async-done | bytes 73744 | tf_op jit(solution)/shard_map/psum | solution.py:58
  305.5 1.4 fusion.26
  306.9 0.4 convolution_multiply_fusion
  307.4 0.1 copy.73
  307.5 0.8 reshape.185
  (17 shorter events, 0.2 us)
Async XLA Ops:
  7.2 112.8 %reduce-scatter.2.cloned.1.call-start = ((), (), s32[]{:S(2)}) async-start(), calls=%async_computation.1 | async-start | bytes 1310720 | tf_op jit(solution)/shard_map/reduce_scatter | solution.py:49
  9.2 66.4 %copy-start = (f32[8,1,8,48,128]{4,3,2,1,0:T(8,128)S(1)}, f32[8,1,8,48,128]{4,3,2,1,0:T(8,128)}, u32[]{:S(2)}) copy-start(f32[8,1,8,48,128]{4,3,2,1,0:T(8,128)} %param.7) | copy-start | bytes 4718596
  77.3 6.9 %copy-start.2 = (s32[8,1,8]{2,1,0:T(1,128)S(1)}, s32[8,1,8]{2,1,0:T(1,128)}, u32[]{:S(2)}) copy-start(s32[8,1,8]{2,1,0:T(1,128)} %param.9) | copy-start | bytes 772
  88.3 64.8 %copy-start.3 = (f32[1,4,128]{2,1,0:T(4,128)S(1)}, f32[1,4,128]{2,1,0:T(4,128)}, u32[]{:S(2)}) copy-start(f32[1,4,128]{2,1,0:T(4,128)} %param.10) | copy-start | bytes 6148
  89.8 63.3 %all-reduce.3.cloned.1.call-start = ((), (), s32[]{:S(2)}) async-start(), calls=%async_computation.2 | async-start | bytes 524288 | tf_op jit(solution)/shard_map/psum | solution.py:50
  120.0 151.8 %all-gather.3.cloned.1.call-start = ((), (), s32[]{:S(2)}) async-start(), calls=%async_computation.4 | async-start | bytes 1310720 | tf_op jit(solution)/shard_map/all_gather | solution.py:52
  243.7 61.8 %all-reduce.5.cloned.1.call-start = ((), (), s32[]{:S(2)}) async-start(), calls=%async_computation.3 | async-start | bytes 393216 | tf_op jit(solution)/shard_map/psum | solution.py:58
  281.1 2.5 copy-start.1
Sparse Core Ops, SparseCore 0:
  89.9 29.9 reduce-scatter.1
  122.3 30.7 all-reduce.2
  243.8 27.9 all-gather.2
  283.6 21.7 all-reduce.4
where the time goes:
time: 315 us
  other arithmetic  154 us (49%)
  waiting for transfers between devices  113 us (36%)
  matrix products  29.1 us (9%)
  between operations  14.1 us (4%)
  local copies, waits for them, and re-layouts  4.08 us (1%)
    another operation x8, other arithmetic, spd_inverse(): factor = jnp.linalg.cholesky(matrix)  82.4 us
    another operation x6, other arithmetic, spd_inverse(): lax.linalg.triangular_solve(factor, identity, left_side=True, lower=True)  69.1 us
    psum x1, waiting for transfers between devices, local(): block_sum = lax.psum(local_sum, 'group')  32.9 us
    reduce_scatter x1, waiting for transfers between devices, local(): lax.psum_scatter(block_table, 'station', scatter_dimension=1, tiled=True)  30.1 us
    all_gather x1, waiting for transfers between devices, local(): segment = lax.all_gather(bias_cov, 'station', axis=1, tiled=True)  27.9 us
    psum x1, waiting for transfers between devices, local(): combined = lax.psum(bias_part.reshape(bias_part.shape[0], -1), 'bias')  21.7 us
    dot_general x1, matrix products, local(): jnp.einsum('shjac,shjad->shjcd', weighted, weighted - solved, precision=p...  6.89 us
  transfers between devices with their start and end apart: 4, of which 4 were waited for; matrix products, arithmetic and copies ran while one was open for 0% of the time, Pallas kernels for 0%

commit v1 on v0

--- a/solution.py
+++ b/solution.py
@@ -55,7 +55,7 @@
     chosen = jnp.einsum("shjx,hxcd->shjcd", local_pick, segment, precision=precise)
     lifted = jnp.einsum("shjac,shjcd->shjad", solved, chosen, precision=precise)
     bias_part = jnp.einsum("shjad,shjbd->sab", lifted, solved, precision=precise)
-    combined = lax.psum(bias_part.reshape(bias_part.shape[0], -1), "bias")
+    combined = jnp.sum(lax.all_gather(bias_part.reshape(bias_part.shape[0], -1), "bias"), axis=0)
     amb_cov = finish_cov(keep_mask, inverse, combined.reshape(bias_part.shape), unimod)
     return (bias_cov, amb_cov)
 

time: 315 us -> 297 us (0.943)
  waiting for transfers between devices: 113 us -> 91 us
  blocking collectives: 0 us -> 5.02 us
    psum x1 -> x0, waiting for transfers between devices: 21.7 us -> none  [local(): combined = lax.psum(bias_part.reshape(bias_part.shape[0], -1), 'bias')]
    all_gather x0 -> x1, blocking collectives: none -> 5.02 us  [local(): lax.all_gather(bias_part.reshape(bias_part.shape[0], -1), 'bias')]
  transfers between devices with their start and end apart: 4 -> 3, of which waited for: 4 -> 3; matrix products, arithmetic and copies ran while one was open for 0% -> 0% of each run, Pallas kernels for 0% -> 0%
where the time goes in v1:
time: 297 us
  other arithmetic  155 us (52%)
  waiting for transfers between devices  91 us (31%)
  matrix products  27.4 us (9%)
  between operations  14.1 us (5%)
  blocking collectives  5.02 us (2%)
  local copies, waits for them, and re-layouts  4.41 us (1%)
    another operation x8, other arithmetic, spd_inverse(): factor = jnp.linalg.cholesky(matrix)  82.4 us
    another operation x6, other arithmetic, spd_inverse(): lax.linalg.triangular_solve(factor, identity, left_side=True, lower=True)  69.3 us
    psum x1, waiting for transfers between devices, local(): block_sum = lax.psum(local_sum, 'group')  32.9 us
    reduce_scatter x1, waiting for transfers between devices, local(): lax.psum_scatter(block_table, 'station', scatter_dimension=1, tiled=True)  30.1 us
    all_gather x1, waiting for transfers between devices, local(): segment = lax.all_gather(bias_cov, 'station', axis=1, tiled=True)  27.9 us
    dot_general x1, matrix products, local(): jnp.einsum('shjac,shjad->shjcd', weighted, weighted - solved, precision=p...  6.9 us
    dot_general x1, matrix products, local(): lifted = jnp.einsum('shjac,shjcd->shjad', solved, chosen, precision=precise)  5.96 us
  transfers between devices with their start and end apart: 3, of which 3 were waited for; matrix products, arithmetic and copies ran while one was open for 0% of the time, Pallas kernels for 0%

profile of v1, /device:TPU:0, one launch (start us, length us, event | category | flops | bytes accessed | tf_op | source)
XLA Modules:
  0.0 296.6 jit_solution(14959452669123224042)
XLA Ops:
  7.2 0.0 reduce-scatter.2.cloned.1.call-start
  7.3 0.7 fusion.43
  8.0 0.1 copy.57
  8.1 1.0 reshape.174
  9.1 0.1 copy.56
  9.2 0.1 fusion.24
  9.3 0.1 copy.58
  9.4 0.1 fusion.30
  9.6 35.2 %custom-call.14 = f32[8,48,48]{2,1,0:T(8,128)S(1)} custom-call(f32[8,48,48]{2,1,0:T(8,128)S(1)} %fusion.30), custom_call_target="Cholesky" | custom-call | tf_op jit(solution)/shard_map/jit(cholesky)/cholesky | solution.py:12
  44.8 0.1 compare_reduce_fusion
  44.9 0.1 select_bitcast_fusion.1
  45.0 29.5 %custom-call.15 = f32[8,1,48,48]{2,3,1,0:T(8,128)S(1)} custom-call(f32[8,1,48,48]{3,2,1,0:T(8,128)S(1)} %select_bitcast_fusion.1), custom_call_target="InvertDiagBlocksLowerTriangular" | custom-call | tf_op jit(solution)/shard_map/triangular_solve | solution.py:14
  74.6 0.5 fusion.28
  75.1 0.5 fusion.44
  75.6 1.7 fusion.10
  77.2 6.9 %fusion.7 = f32[8,8,128,128]{3,2,1,0:T(8,128)S(1)} fusion(f32[8,8,128,48]{2,3,1,0:T(8,128)S(1)} %fusion.10, f32[8,1,8,48,128]{4,3,2,1,0:T(8,128)S(1)} %copy-done, f32[8,48]{1,0:T(8,128)S(1)} %fusion.43), kind=kOutput, calls=%fused_computation.9 | convolution fusion | flops 605159424 | bytes 7341568 | tf_op jit(solution)/shard_map/shjac,shjad->shjcd/dot_general | solution.py:43
  84.2 4.1 %fusion.12 = f32[16,128,128]{2,0,1:T(8,128)S(1)} fusion(f32[8,8,128,128]{3,2,1,0:T(8,128)S(1)} %fusion.7, s32[8,8]{1,0:T(8,128)S(1)} %bitcast.87), kind=kOutput, calls=%fused_computation.14 | convolution fusion | flops 201327616 | bytes 5243136 | tf_op jit(solution)/shard_map/shjx,shjcd->hxcd/dot_general | solution.py:48
  88.3 1.4 copy.63
  89.7 0.0 reduce-scatter.2.cloned.1.call-update
  89.7 0.0 all-reduce.2.cloned.1.call-start
  89.8 30.1 %reduce-scatter.2.cloned.1.call-done = f32[1,4,128,128]{2,3,1,0:T(8,128)} async-done(((f32[1,16,128,128]{2,3,1,0:T(8,128)}), f32[1,4,128,128]{2,3,1,0:T(8,128)}) %reduce-scatter.2.cloned.1.call-update) | async-done | bytes 262160 | tf_op jit(solution)/shard_map/reduce_scatter | solution.py:49
  119.9 0.0 all-reduce.2.cloned.1.call-update
  119.9 0.0 all-gather.3.cloned.1.call-start
  120.0 0.1 copy.64
  120.1 32.9 %all-reduce.2.cloned.1.call-done = f32[1,4,128,128]{2,3,1,0:T(8,128)} async-done(((f32[1,4,128,128]{2,3,1,0:T(8,128)}), f32[1,4,128,128]{2,3,1,0:T(8,128)}) %all-reduce.2.cloned.1.call-update) | async-done | bytes 262160 | tf_op jit(solution)/shard_map/psum | solution.py:50
  153.1 1.0 multiply_add_fusion
  154.0 0.1 copy.65
  154.2 1.0 fusion.23
  155.2 46.9 %custom-call.16 = f32[1,4,128,128]{3,2,1,0:T(8,128)S(1)} custom-call(f32[1,4,128,128]{3,2,1,0:T(8,128)S(1)} %fusion.23), custom_call_target="Cholesky" | custom-call | tf_op jit(solution)/shard_map/jit(cholesky)/cholesky | solution.py:12
  202.1 0.1 compare_reduce_fusion.1
  202.2 0.1 select_bitcast_fusion
  202.3 39.5 %custom-call.17 = f32[1,4,1,128,128]{3,4,2,1,0:T(8,128)S(1)} custom-call(f32[1,4,1,128,128]{4,3,2,1,0:T(8,128)S(1)} %select_bitcast_fusion), custom_call_target="InvertDiagBlocksLowerTriangular" | custom-call | tf_op jit(solution)/shard_map/triangular_solve | solution.py:14
  241.9 0.6 fusion.21
  242.5 1.3 fusion.45
  243.8 0.1 copy.70
  244.0 0.1 convert_element_type.47
  244.1 27.9 %all-gather.3.cloned.1.call-done = f32[16,128,128]{2,1,0:T(8,128)} async-done(((f32[4,128,128]{2,1,0:T(8,128)}), f32[16,128,128]{2,1,0:T(8,128)}) %all-gather.3.cloned.1.call-update) | async-done | bytes 1048592 | tf_op jit(solution)/shard_map/all_gather | solution.py:52
  272.0 3.3 %convolution_bitcast_fusion = f32[8,8,128,128]{3,1,0,2:T(8,128)S(1)} fusion(f32[16,128,128,1]{2,1,0,3:T(8,128)} %bitcast.86, s32[8,8]{1,0:T(8,128)S(1)} %bitcast.88), kind=kOutput, calls=%fused_computation.4 | convolution fusion | flops 201327616 | bytes 5243136 | tf_op jit(solution)/shard_map/shjx,hxcd->shjcd/dot_general | solution.py:55
  275.3 6.0 %fusion = f32[8,8,48,128]{3,2,1,0:T(8,128)S(1)} fusion(f32[8,8,128,48]{2,3,1,0:T(8,128)S(1)} %fusion.10, f32[8,8,128,128]{3,1,0,2:T(8,128)S(1)} %convolution_bitcast_fusion), kind=kOutput, calls=%fused_computation | convolution fusion | flops 603979776 | bytes 7340032 | tf_op jit(solution)/shard_map/shjac,shjcd->shjad/dot_general | solution.py:56
  281.2 1.6 fusion.15
  282.8 0.1 all_gather_reshape.3
  283.0 5.0 %all_gather.7 = f32[2,8,2304]{2,1,0:T(8,128)S(1)} all-gather(f32[1,8,2304]{2,1,0:T(8,128)S(1)} %all_gather_reshape.3), channel_id=1, replica_groups=mesh['station'=4,'group'=4,'bias'=2] {'bias'}, dimensions={0}, use_global_device_ids=true | all-gather | bytes 221184 | tf_op jit(solution)/shard_map/all_gather | solution.py:58
  288.0 0.1 reshape.180
  288.1 0.1 copy.71
  288.2 0.5 fusion.26
  288.8 0.4 convolution_multiply_fusion
  289.2 0.1 copy.74
  289.3 0.8 reshape.181
  (19 shorter events, 0.2 us)
Async XLA Ops:
  7.2 112.7 %reduce-scatter.2.cloned.1.call-start = ((), (), s32[]{:S(2)}) async-start(), calls=%async_computation.1 | async-start | bytes 1310720 | tf_op jit(solution)/shard_map/reduce_scatter | solution.py:49
  9.2 66.4 %copy-start = (f32[8,1,8,48,128]{4,3,2,1,0:T(8,128)S(1)}, f32[8,1,8,48,128]{4,3,2,1,0:T(8,128)}, u32[]{:S(2)}) copy-start(f32[8,1,8,48,128]{4,3,2,1,0:T(8,128)} %param.7) | copy-start | bytes 4718596
  77.2 6.9 %copy-start.2 = (s32[8,1,8]{2,1,0:T(1,128)S(1)}, s32[8,1,8]{2,1,0:T(1,128)}, u32[]{:S(2)}) copy-start(s32[8,1,8]{2,1,0:T(1,128)} %param.9) | copy-start | bytes 772
  88.3 64.8 %copy-start.3 = (f32[1,4,128]{2,1,0:T(4,128)S(1)}, f32[1,4,128]{2,1,0:T(4,128)}, u32[]{:S(2)}) copy-start(f32[1,4,128]{2,1,0:T(4,128)} %param.10) | copy-start | bytes 6148
  89.7 63.3 %all-reduce.2.cloned.1.call-start = ((), (), s32[]{:S(2)}) async-start(), calls=%async_computation.2 | async-start | bytes 524288 | tf_op jit(solution)/shard_map/psum | solution.py:50
  119.9 152.0 %all-gather.3.cloned.1.call-start = ((), (), s32[]{:S(2)}) async-start(), calls=%async_computation.3 | async-start | bytes 1310720 | tf_op jit(solution)/shard_map/all_gather | solution.py:52
  155.2 88.8 %copy-start.1 = (s32[8,2304]{1,0:T(8,128)S(1)}, s32[8,2304]{1,0:T(8,128)}, u32[]{:S(2)}) copy-start(s32[8,2304]{1,0:T(8,128)} %param.11) | copy-start | bytes 221188
Sparse Core Ops, SparseCore 0:
  89.9 29.9 reduce-scatter.1
  122.2 30.7 all-reduce.1
  243.9 27.9 all-gather.2
